TPU v7x, 32 devices: a whole 2x2x4 slice. The times are simulated.
32 devices in a mesh: rows: 4 (over x, core), cols: 8 (over z, y).
Axes of the slice: x: 2, y: 2, z: 4, core: 2. Of those that a mesh axis runs over, the one named last changes fastest.
Arguments:
- tensor: float32 [48, 256, 512], P('rows', 'cols'), may hold values from 0 to 1
- first_factor: float32 [48, 256], P('rows', 'cols'), may hold values from -2.5 to 2.5
- second_factor: float32 [256, 256], P('cols', 'rows'), may hold values from -2.5 to 2.5
- third_factor: float32 [512, 256], P(('rows', 'cols')), may hold values from -2.5 to 2.5
Outputs:
- first_new: float32 [48, 256], P('rows', 'cols')
- second_new: float32 [256, 256], P('cols', 'rows')
- third_new: float32 [512, 256], P(('rows', 'cols'))
All inputs are finite; a program needn't handle non-finite values.
Results may differ from a plain program's by a relative error of at most 0.0003.
Values sent between devices are 32-bit elements; how exact they have to be, the bound alone decides.
A program may use at most 64 MiB of HBM per device.

v0:
```python
import jax
import jax.numpy as jnp
from jax import lax
from jax.sharding import PartitionSpec as P

STEPS = 2


def gather_third(piece):
    return lax.all_gather(piece, ("rows", "cols"), axis=0, tiled=True)


def per_device(tensor, first_factor, second_factor, third_factor):
    high = lax.Precision.HIGHEST
    rows_dev, cols_dev, depth = tensor.shape
    size_i = rows_dev * lax.axis_size("rows")
    size_j = cols_dev * lax.axis_size("cols")
    rate_a = 4.0 / jnp.sqrt(jnp.float32(size_j * depth))
    rate_b = 4.0 / jnp.sqrt(jnp.float32(size_i * depth))
    rate_c = 4.0 / jnp.sqrt(jnp.float32(size_i * size_j))
    flat_target = tensor.reshape(-1, depth)
    shard_a, shard_b = (first_factor, second_factor)
    whole_c = gather_third(third_factor)
    for step_index in range(STEPS):
        whole_a = lax.all_gather(shard_a, "cols", axis=1, tiled=True)
        whole_b = lax.all_gather(shard_b, "rows", axis=1, tiled=True)
        khatri = (whole_a[:, None, :] * whole_b[None, :, :]).reshape(-1, whole_a.shape[1])
        model_tile = jnp.dot(khatri, whole_c.T, precision=high, preferred_element_type=jnp.float32)
        deriv = jax.nn.sigmoid(model_tile) - flat_target
        deriv_c = jnp.dot(
            deriv, whole_c, precision=high, preferred_element_type=jnp.float32
        ).reshape(rows_dev, cols_dev, -1)
        term_a = jnp.einsum("ijr,jr->ir", deriv_c, whole_b, precision=high)
        term_b = jnp.einsum("ijr,ir->jr", deriv_c, whole_a, precision=high)
        term_c = lax.dot_general(
            deriv,
            khatri,
            (((0,), (0,)), ((), ())),
            precision=high,
            preferred_element_type=jnp.float32,
        )
        shard_a = shard_a - rate_a * lax.psum_scatter(
            term_a, "cols", scatter_dimension=1, tiled=True
        )
        shard_b = shard_b - rate_b * lax.psum_scatter(
            term_b, "rows", scatter_dimension=1, tiled=True
        )
        whole_c = whole_c - rate_c * lax.psum(term_c, ("rows", "cols"))
    owner = lax.axis_index("rows") * lax.axis_size("cols") + lax.axis_index("cols")
    count = third_factor.shape[0]
    shard_c = lax.dynamic_slice_in_dim(whole_c, owner * count, count, 0)
    return (shard_a, shard_b, shard_c)


def solution(mesh):
    in_specs = (
        P("rows", "cols", None),
        P("rows", "cols"),
        P("cols", "rows"),
        P(("rows", "cols"), None),
    )
    out_specs = (P("rows", "cols"), P("cols", "rows"), P(("rows", "cols"), None))
    return jax.shard_map(
        per_device, mesh=mesh, in_specs=in_specs, out_specs=out_specs, check_vma=False
    )
```

profile of v0, /device:TPU:0, one launch (start us, length us, event | category | flops | bytes accessed | tf_op | source)
XLA Modules:
  0.0 396.7 jit_solution(13207134595895252881)
XLA Ops:
  8.0 0.0 reduce-scatter.13.cloned.1.call-start
  8.0 6.5 %all-gather.1 = f32[4,64,32]{1,2,0:T(8,128)S(1)} all-gather(f32[1,64,32]{1,2,0:T(8,128)} %bitcast.87), channel_id=1, replica_groups=mesh['rows'=4,'cols'=8] {'rows'}, dimensions={0}, use_global_device_ids=true | all-gather | bytes 40960 | tf_op jit(solution)/shard_map/all_gather | solution.py:26
  14.5 0.0 copy-start.1
  14.6 0.1 reshape.33
  14.7 0.6 copy-done.1
  15.2 31.3 %all-gather = f32[8,32,12]{1,2,0:T(8,128)S(1)} all-gather(f32[1,32,12]{1,2,0:T(8,128)S(1)} %bitcast.90), channel_id=1, replica_groups=mesh['rows'=4,'cols'=8] {'cols'}, dimensions={0}, use_global_device_ids=true | all-gather | bytes 13824 | tf_op jit(solution)/shard_map/all_gather | solution.py:25
  46.6 0.0 copy-start.2
  46.6 0.0 copy-start.3
  46.6 0.1 reshape.31
  46.7 0.6 copy-done.2
  47.3 68.2 %all_gather.17 = f32[512,256]{1,0:T(8,128)S(1)} all-gather(f32[16,256]{1,0:T(8,128)S(1)} %copy-done.2), channel_id=1, replica_groups=mesh['rows'=4,'cols'=8] {'rows','cols'}, dimensions={0}, use_global_device_ids=true | all-gather | bytes 540672 | tf_op jit(solution)/shard_map/all_gather | solution.py:10
  115.6 0.0 copy-done.3
  115.6 0.9 fusion.7
  116.5 0.8 fusion.10
  117.3 0.1 multiply_reduce_fusion.3
  117.4 0.8 copy.42
  118.1 0.0 reduce-scatter.13.cloned.1.call-update
  118.2 0.0 reduce-scatter.15.cloned.1.call-start
  118.3 0.7 copy.44
  119.0 0.0 reduce-scatter.15.cloned.1.call-update
  119.0 0.0 all-reduce.3.cloned.1.call-start
  119.1 2.3 fusion.11
  121.4 0.0 all-reduce.3.cloned.1.call-update
  121.4 0.0 reduce-scatter.17.cloned.1.call-start
  121.4 55.9 %reduce-scatter.13.cloned.1.call-done = f32[32,12]{1,0:T(8,128)} async-done(((f32[256,12]{1,0:T(8,128)}), f32[32,12]{1,0:T(8,128)}) %reduce-scatter.13.cloned.1.call-update) | async-done | bytes 1552
  177.3 0.8 copy.43
  178.1 30.5 %all-gather.3 = f32[8,32,12]{1,2,0:T(8,128)S(1)} all-gather(f32[1,32,12]{1,2,0:T(8,128)S(1)} %fusion.9), channel_id=1, replica_groups=mesh['rows'=4,'cols'=8] {'cols'}, dimensions={0}, use_global_device_ids=true | all-gather | bytes 13824 | tf_op jit(solution)/shard_map/all_gather | solution.py:25
  208.7 0.1 reshape.37
  208.7 0.0 reduce-scatter.15.cloned.1.call-done
  208.7 0.0 copy-start
  208.7 0.8 copy.45
  209.6 0.0 copy-done
  209.6 5.2 %all-gather.2 = f32[4,64,32]{1,2,0:T(8,128)S(1)} all-gather(f32[1,64,32]{1,2,0:T(8,128)S(1)} %fusion.8), channel_id=1, replica_groups=mesh['rows'=4,'cols'=8] {'rows'}, dimensions={0}, use_global_device_ids=true | all-gather | bytes 40960 | tf_op jit(solution)/shard_map/all_gather | solution.py:26
  214.9 0.1 reshape.35
  215.0 35.3 %all-reduce.3.cloned.1.call-done = f32[512,256]{1,0:T(8,128)} async-done(((f32[512,256]{1,0:T(8,128)}), f32[512,256]{1,0:T(8,128)}) %all-reduce.3.cloned.1.call-update) | async-done | bytes 524304 | tf_op jit(solution)/shard_map/psum | solution.py:48
  250.3 1.2 multiply_subtract_fusion
  251.5 0.9 fusion.6
  252.4 0.8 fusion.12
  253.2 0.1 multiply_reduce_fusion.1
  253.2 0.8 copy.46
  254.0 0.0 reduce-scatter.17.cloned.1.call-update
  254.0 0.0 reduce-scatter.19.cloned.1.call-start
  254.1 0.8 copy.48
  254.9 0.0 reduce-scatter.19.cloned.1.call-update
  254.9 0.0 all-reduce.5.cloned.1.call-start
  255.0 2.2 fusion.13
  257.2 0.0 all-reduce.5.cloned.1.call-update
  257.2 58.0 %reduce-scatter.17.cloned.1.call-done = f32[32,12]{1,0:T(8,128)} async-done(((f32[256,12]{1,0:T(8,128)}), f32[32,12]{1,0:T(8,128)}) %reduce-scatter.17.cloned.1.call-update) | async-done | bytes 1552
  315.2 0.8 copy.47
  316.0 0.6 multiply_subtract_fusion.3
  316.6 19.6 %reduce-scatter.19.cloned.1.call-done = f32[64,32]{1,0:T(8,128)} async-done(((f32[256,32]{1,0:T(8,128)}), f32[64,32]{1,0:T(8,128)}) %reduce-scatter.19.cloned.1.call-update) | async-done | bytes 8208
  336.2 0.8 copy.49
  337.0 0.6 multiply_subtract_fusion.1
  337.6 50.6 %all-reduce.5.cloned.1.call-done = f32[512,256]{1,0:T(8,128)} async-done(((f32[512,256]{1,0:T(8,128)}), f32[512,256]{1,0:T(8,128)}) %all-reduce.5.cloned.1.call-update) | async-done | bytes 524304 | tf_op jit(solution)/shard_map/psum | solution.py:48
  388.2 1.3 dynamic-slice_subtract_fusion
  (10 shorter events, 0.3 us)
Async XLA Ops:
  8.0 169.3 %reduce-scatter.13.cloned.1.call-start = ((), (), s32[]{:S(2)}) async-start(), calls=%async_computation.6 | async-start | bytes 147456
  14.5 0.7 copy-start.1
  46.6 0.7 copy-start.2
  46.6 68.9 %copy-start.3 = (f32[12,32,512]{2,1,0:T(8,128)S(1)}, f32[12,32,512]{2,1,0:T(8,128)}, u32[]{:S(2)}) copy-start(f32[12,32,512]{2,1,0:T(8,128)} %param.4) | copy-start | bytes 2359300
  118.2 90.6 %reduce-scatter.15.cloned.1.call-start = ((), (), s32[]{:S(2)}) async-start(), calls=%async_computation.7 | async-start | bytes 163840
  119.0 131.3 %all-reduce.3.cloned.1.call-start = ((), (), s32[]{:S(2)}) async-start(), calls=%async_computation.4 | async-start | bytes 1048576 | tf_op jit(solution)/shard_map/psum | solution.py:48
  121.4 193.8 %reduce-scatter.17.cloned.1.call-start = ((), (), s32[]{:S(2)}) async-start(), calls=%async_computation.8 | async-start | bytes 147456
  208.7 0.8 copy-start
  254.0 82.1 %reduce-scatter.19.cloned.1.call-start = ((), (), s32[]{:S(2)}) async-start(), calls=%async_computation.9 | async-start | bytes 163840
  254.9 133.3 %all-reduce.5.cloned.1.call-start = ((), (), s32[]{:S(2)}) async-start(), calls=%async_computation.5 | async-start | bytes 1048576 | tf_op jit(solution)/shard_map/psum | solution.py:48
Sparse Core Ops, SparseCore 0:
  118.3 58.9 reduce-scatter.12
  179.7 18.6 reduce-scatter.14
  254.2 60.9 reduce-scatter.16
  317.5 18.6 reduce-scatter.18
Sparse Core Ops, SparseCore 1:
  124.8 125.5 all-reduce.2
  260.7 127.5 all-reduce.4
where the time goes:
time: 397 us
  waiting for transfers between devices  219 us (55%)
  blocking collectives  142 us (36%)
  between operations  15.4 us (4%)
  local copies, waits for them, and re-layouts  7.98 us (2%)
  matrix products  7.96 us (2%)
  other arithmetic  3.99 us (1%)
    unnamed x10, waiting for transfers between devices  133 us
    psum x2, waiting for transfers between devices, per_device(): whole_c = whole_c - rate_c * lax.psum(term_c, ('rows', 'cols'))  85.9 us
    all_gather x1, blocking collectives, gather_third(): return lax.all_gather(piece, ('rows', 'cols'), axis=0, tiled=True)  68.2 us
    all_gather x2, blocking collectives, per_device(): whole_a = lax.all_gather(shard_a, 'cols', axis=1, tiled=True)  61.9 us
    all_gather x2, blocking collectives, per_device(): whole_b = lax.all_gather(shard_b, 'rows', axis=1, tiled=True)  11.7 us
  transfers between devices with their start and end apart: 6, of which 5 were waited for; matrix products, arithmetic and copies ran while one was open for 3% of the time, Pallas kernels for 0%

commit v1 on v0

--- a/solution.py
+++ b/solution.py
@@ -6,8 +6,21 @@
 STEPS = 2
 
 
+def fit_row(block_here):
+    axis_tag = ("rows", "cols")
+    placed, v1 = (lax.axis_size(axis_tag), lax.axis_index(axis_tag))
+    mat_out, aux = (block_here, 1)
+    while aux < placed:
+        side_arr = lax.ppermute(mat_out, axis_tag, tuple(((ix, ix ^ aux) for ix in range(placed))))
+        later = jnp.concatenate([mat_out, side_arr], axis=0)
+        r2 = jnp.concatenate([side_arr, mat_out], axis=0)
+        mat_out = jnp.where(v1 & aux == 0, later, r2)
+        aux = 2 * aux
+    return mat_out
+
+
 def gather_third(piece):
-    return lax.all_gather(piece, ("rows", "cols"), axis=0, tiled=True)
+    return fit_row(piece)
 
 
 def per_device(tensor, first_factor, second_factor, third_factor):

time: 397 us -> 352 us (0.89)
  blocking collectives: 142 us -> 75.3 us
  waiting for transfers between devices: 219 us -> 231 us
  starting transfers between devices: 0.25 us -> 10.5 us
    all_gather x1 -> x0, blocking collectives: 68.2 us -> none  [gather_third(): return lax.all_gather(piece, ('rows', 'cols'), axis=0, tiled=True)]
    ppermute x0 -> x5, starting transfers between devices: none -> 10.3 us  [fit_row(): lax.ppermute(mat_out, axis_tag, tuple(((ix, ix ^ aux) for ix in range(pla...]
    ppermute x0 -> x5, waiting for transfers between devices: none -> 7.4 us  [fit_row(): lax.ppermute(mat_out, axis_tag, tuple(((ix, ix ^ aux) for ix in range(pla...]
  transfers between devices with their start and end apart: 6 -> 11, of which waited for: 5 -> 9; matrix products, arithmetic and copies ran while one was open for 3% -> 3% of each run, Pallas kernels for 0% -> 0%
where the time goes in v1:
time: 352 us; the launch traced here: 351 us
  waiting for transfers between devices  231 us (66%)
  blocking collectives  75.3 us (21%)
  between operations  15.4 us (4%)
  starting transfers between devices  10.5 us (3%)
  matrix products  7.99 us (2%)
  local copies, waits for them, and re-layouts  7.35 us (2%)
  other arithmetic  4.02 us (1%)
    unnamed x10, waiting for transfers between devices  137 us
    psum x2, waiting for transfers between devices, per_device(): whole_c = whole_c - rate_c * lax.psum(term_c, ('rows', 'cols'))  85.9 us
    all_gather x2, blocking collectives, per_device(): whole_a = lax.all_gather(shard_a, 'cols', axis=1, tiled=True)  62.3 us
    all_gather x2, blocking collectives, per_device(): whole_b = lax.all_gather(shard_b, 'rows', axis=1, tiled=True)  13 us
    ppermute x5, starting transfers between devices, fit_row(): lax.ppermute(mat_out, axis_tag, tuple(((ix, ix ^ aux) for ix in range(pla...  10.3 us
    ppermute x5, waiting for transfers between devices, fit_row(): lax.ppermute(mat_out, axis_tag, tuple(((ix, ix ^ aux) for ix in range(pla...  7.4 us
    unnamed x20, local copies, waits for them, and re-layouts  7.23 us
  transfers between devices with their start and end apart: 11, of which 9 were waited for; matrix products, arithmetic and copies ran while one was open for 3% of the time, Pallas kernels for 0%

profile of v1, /device:TPU:0, one launch (start us, length us, event | category | flops | bytes accessed | tf_op | source)
XLA Modules:
  0.0 351.2 jit_solution(11944969352527034032)
XLA Ops:
  8.0 0.0 copy-start.2
  8.0 0.0 reduce-scatter.13.cloned.1.call-start
  8.1 3.1 collective-permute-start
  11.1 1.9 collective-permute-done
  13.0 0.0 copy-done.2
  13.1 2.1 collective-permute-start.1
  15.2 1.9 collective-permute-done.1
  17.1 3.1 collective-permute-start.2
  20.2 2.2 collective-permute-done.2
  22.4 0.0 copy-start.3
  22.5 0.1 collective-permute-start.3
  22.5 1.3 collective-permute-done.3
  23.9 0.0 copy-start
  23.9 1.9 collective-permute-start.4
  25.8 0.0 copy-done
  25.8 7.8 %all-gather.1 = f32[4,64,32]{1,2,0:T(8,128)S(1)} all-gather(f32[1,64,32]{1,2,0:T(8,128)S(1)} %bitcast.85), channel_id=1, replica_groups=mesh['rows'=4,'cols'=8] {'rows'}, dimensions={0}, use_global_device_ids=true | all-gather | bytes 40960 | tf_op jit(solution)/shard_map/all_gather | solution.py:39
  33.6 0.0 copy-start.1
  33.6 0.1 reshape.33
  33.8 0.6 copy-done.1
  34.3 31.7 %all-gather = f32[8,32,12]{1,2,0:T(8,128)S(1)} all-gather(f32[1,32,12]{1,2,0:T(8,128)S(1)} %bitcast.88), channel_id=1, replica_groups=mesh['rows'=4,'cols'=8] {'cols'}, dimensions={0}, use_global_device_ids=true | all-gather | bytes 13824 | tf_op jit(solution)/shard_map/all_gather | solution.py:38
  66.1 0.1 reshape.31
  66.2 0.0 collective-permute-done.4
  66.2 0.0 copy-done.3
  66.2 1.0 fusion.7
  67.2 0.8 fusion.8
  68.0 0.1 multiply_reduce_fusion.3
  68.0 0.8 copy.42
  68.8 0.0 reduce-scatter.13.cloned.1.call-update
  68.8 0.0 reduce-scatter.15.cloned.1.call-start
  68.9 0.7 copy.44
  69.7 0.0 reduce-scatter.15.cloned.1.call-update
  69.7 0.0 all-reduce.3.cloned.1.call-start
  69.7 2.3 fusion.13
  72.0 0.0 all-reduce.3.cloned.1.call-update
  72.0 0.0 reduce-scatter.17.cloned.1.call-start
  72.1 59.8 %reduce-scatter.13.cloned.1.call-done = f32[32,12]{1,0:T(8,128)} async-done(((f32[256,12]{1,0:T(8,128)}), f32[32,12]{1,0:T(8,128)}) %reduce-scatter.13.cloned.1.call-update) | async-done | bytes 1552
  131.9 0.8 copy.43
  132.7 30.6 %all-gather.3 = f32[8,32,12]{1,2,0:T(8,128)S(1)} all-gather(f32[1,32,12]{1,2,0:T(8,128)S(1)} %fusion.10), channel_id=1, replica_groups=mesh['rows'=4,'cols'=8] {'cols'}, dimensions={0}, use_global_device_ids=true | all-gather | bytes 13824 | tf_op jit(solution)/shard_map/all_gather | solution.py:38
  163.2 0.1 reshape.37
  163.3 0.0 reduce-scatter.15.cloned.1.call-done
  163.3 0.8 copy.45
  164.2 5.2 %all-gather.2 = f32[4,64,32]{1,2,0:T(8,128)S(1)} all-gather(f32[1,64,32]{1,2,0:T(8,128)S(1)} %fusion.9), channel_id=1, replica_groups=mesh['rows'=4,'cols'=8] {'rows'}, dimensions={0}, use_global_device_ids=true | all-gather | bytes 40960 | tf_op jit(solution)/shard_map/all_gather | solution.py:39
  169.4 0.1 reshape.35
  169.6 35.2 %all-reduce.3.cloned.1.call-done = f32[512,256]{1,0:T(8,128)} async-done(((f32[512,256]{1,0:T(8,128)}), f32[512,256]{1,0:T(8,128)}) %all-reduce.3.cloned.1.call-update) | async-done | bytes 524304 | tf_op jit(solution)/shard_map/psum | solution.py:61
  204.8 1.2 multiply_subtract_fusion
  206.0 0.9 fusion.6
  206.9 0.8 fusion.14
  207.7 0.1 multiply_reduce_fusion.1
  207.8 0.8 copy.46
  208.5 0.0 reduce-scatter.17.cloned.1.call-update
  208.6 0.0 reduce-scatter.19.cloned.1.call-start
  208.6 0.8 copy.48
  209.4 0.0 reduce-scatter.19.cloned.1.call-update
  209.4 0.0 all-reduce.5.cloned.1.call-start
  209.5 2.2 fusion.15
  211.7 0.0 all-reduce.5.cloned.1.call-update
  211.7 58.0 %reduce-scatter.17.cloned.1.call-done = f32[32,12]{1,0:T(8,128)} async-done(((f32[256,12]{1,0:T(8,128)}), f32[32,12]{1,0:T(8,128)}) %reduce-scatter.17.cloned.1.call-update) | async-done | bytes 1552
  269.7 0.8 copy.47
  270.5 0.6 multiply_subtract_fusion.3
  271.1 19.5 %reduce-scatter.19.cloned.1.call-done = f32[64,32]{1,0:T(8,128)} async-done(((f32[256,32]{1,0:T(8,128)}), f32[64,32]{1,0:T(8,128)}) %reduce-scatter.19.cloned.1.call-update) | async-done | bytes 8208
  290.7 0.8 copy.49
  291.5 0.6 multiply_subtract_fusion.1
  292.1 50.7 %all-reduce.5.cloned.1.call-done = f32[512,256]{1,0:T(8,128)} async-done(((f32[512,256]{1,0:T(8,128)}), f32[512,256]{1,0:T(8,128)}) %all-reduce.5.cloned.1.call-update) | async-done | bytes 524304 | tf_op jit(solution)/shard_map/psum | solution.py:61
  342.8 1.3 dynamic-slice_subtract_fusion
  (14 shorter events, 0.3 us)
Async XLA Ops:
  8.0 5.0 %copy-start.2 = (f32[16,256]{1,0:T(8,128)S(1)}, f32[16,256]{1,0:T(8,128)}, u32[]{:S(2)}) copy-start(f32[16,256]{1,0:T(8,128)} %param.7) | copy-start | bytes 49156
  8.0 123.8 %reduce-scatter.13.cloned.1.call-start = ((), (), s32[]{:S(2)}) async-start(), calls=%async_computation.6 | async-start | bytes 147456
  8.1 5.0 %collective-permute-start = (f32[16,256]{1,0:T(8,128)}, f32[16,256]{1,0:T(8,128)S(1)}, u32[]{:S(2)}, u32[]{:S(2)}) collective-permute-start(f32[16,256]{1,0:T(8,128)} %param.7), channel_id=1, source_target_pairs={{0,1},{1,0},{2,3},{3,2},{4,5},{5,4},{6,7},{7,6},{8,9},{9,8},{10,11... | collective-permute-start | bytes 49160 | tf_op jit(solution)/shard_map/ppermute | solution.py:14
  13.1 4.0 %collective-permute-start.1 = (f32[32,256]{1,0:T(8,128)S(1)}, f32[32,256]{1,0:T(8,128)S(1)}, u32[]{:S(2)}, u32[]{:S(2)}) collective-permute-start(f32[32,256]{1,0:T(8,128)S(1)} %maximum_select_fusion.6), channel_id=1, source_target_pairs={{0,2},{1,3},{2,0},{3,1},{4,6},{5,7},{6,4},{7,5},{8,10},{9,11},{10,... | collective-permute-start | bytes 98312 | tf_op jit(solution)/shard_map/ppermute | solution.py:14
  17.1 5.3 %collective-permute-start.2 = (f32[64,256]{1,0:T(8,128)S(1)}, f32[64,256]{1,0:T(8,128)S(1)}, u32[]{:S(2)}, u32[]{:S(2)}) collective-permute-start(f32[64,256]{1,0:T(8,128)S(1)} %maximum_select_fusion.5), channel_id=1, source_target_pairs={{0,4},{1,5},{2,6},{3,7},{4,0},{5,1},{6,2},{7,3},{8,12},{9,13},{10,... | collective-permute-start | bytes 196616 | tf_op jit(solution)/shard_map/ppermute | solution.py:14
  22.4 43.7 %copy-start.3 = (f32[12,32,512]{2,1,0:T(8,128)S(1)}, f32[12,32,512]{2,1,0:T(8,128)}, u32[]{:S(2)}) copy-start(f32[12,32,512]{2,1,0:T(8,128)} %param.4) | copy-start | bytes 2359300
  22.5 1.4 collective-permute-start.3
  23.9 1.9 copy-start
  23.9 42.3 %collective-permute-start.4 = (f32[256,256]{1,0:T(8,128)S(1)}, f32[256,256]{1,0:T(8,128)S(1)}, u32[]{:S(2)}, u32[]{:S(2)}) collective-permute-start(f32[256,256]{1,0:T(8,128)S(1)} %maximum_select_fusion.1), channel_id=1, source_target_pairs={{0,16},{1,17},{2,18},{3,19},{4,20},{5,21},{6,22},{7,23},{8,24},{9,... | collective-permute-start | bytes 786440 | tf_op jit(solution)/shard_map/ppermute | solution.py:14
  33.6 0.7 copy-start.1
  68.8 94.5 %reduce-scatter.15.cloned.1.call-start = ((), (), s32[]{:S(2)}) async-start(), calls=%async_computation.7 | async-start | bytes 163840
  69.7 135.1 %all-reduce.3.cloned.1.call-start = ((), (), s32[]{:S(2)}) async-start(), calls=%async_computation.4 | async-start | bytes 1048576 | tf_op jit(solution)/shard_map/psum | solution.py:61
  72.0 197.7 %reduce-scatter.17.cloned.1.call-start = ((), (), s32[]{:S(2)}) async-start(), calls=%async_computation.8 | async-start | bytes 147456
  208.6 82.1 %reduce-scatter.19.cloned.1.call-start = ((), (), s32[]{:S(2)}) async-start(), calls=%async_computation.9 | async-start | bytes 163840
  209.4 133.4 %all-reduce.5.cloned.1.call-start = ((), (), s32[]{:S(2)}) async-start(), calls=%async_computation.5 | async-start | bytes 1048576 | tf_op jit(solution)/shard_map/psum | solution.py:61
Sparse Core Ops, SparseCore 0:
  68.9 62.8 reduce-scatter.12
  134.3 18.6 reduce-scatter.14
  208.7 61.0 reduce-scatter.16
  272.0 18.6 reduce-scatter.18
Sparse Core Ops, SparseCore 1:
  75.4 129.3 all-reduce.2
  215.2 127.5 all-reduce.4
